TPU v7x, 256 devices: a whole 4x4x8 slice. The times are simulated.
256 devices in a mesh: ctx: 32 (over x, y, z_lo), tp: 8 (over z_hi, core).
Axes of the slice: x: 4, y: 4, z: 8 (z_hi: 4, z_lo: 2; z = z_hi * 2 + z_lo), core: 2. Of those that a mesh axis runs over, the one named last changes fastest.
Arguments:
- features: bfloat16 [8192, 8192], P('ctx', 'tp'), may hold values from -6 to 6
- inner: bfloat16 [8192, 8192], P('ctx', 'tp'), may hold values from -6 to 6
- w_bc: bfloat16 [8192, 2, 1024], P('ctx', None, 'tp'), may hold values from -0.005859375 to 0.005859375
- w_dt: bfloat16 [8192, 128], P('ctx', 'tp'), may hold values from -0.0625 to 0.0625
- dt_bias: float32 [128], P('tp'), may hold values from -4 to 0
- decay_rate: float32 [128], P('tp'), may hold values from 0.00012207031 to 1
- skip: float32 [128], P('tp'), may hold values from 0.5 to 1.5
- cotangent: bfloat16 [8192, 8192], P('ctx', 'tp'), may hold values from -6 to 6
- fisher: float32 [8192, 2, 1024], P('ctx', None, 'tp'), may hold values from 0.5 to 4
- importance: float32 [8192, 2, 1024], P('ctx', None, 'tp'), may hold values from 0 to 10
Outputs:
- outputs: bfloat16 [8192, 8192], P('ctx', 'tp')
- grad_inner: bfloat16 [8192, 8192], P('ctx', 'tp')
- grad_features: bfloat16 [8192, 8192], P('ctx', 'tp')
- weight_new: float32 [8192, 2, 1024], P('ctx', None, 'tp')
- fisher_new: float32 [8192, 2, 1024], P('ctx', None, 'tp')
- importance_new: float32 [8192, 2, 1024], P('ctx', None, 'tp')
All inputs are finite; a program needn't handle non-finite values.
Results may differ from a plain program's by a relative error of at most 0.014.
Values may be sent and summed in bfloat16 or wider, within the bound.
A program may use at most 128 MiB of HBM per device.

v0:
```python
from functools import partial
import math
import jax
import jax.numpy as jnp
from jax import lax
from jax.sharding import Mesh
from jax.sharding import PartitionSpec as P

HEADS = 128
P_SIZE = 64
N = 128
G = 8
SPAN = 256
CTX = ("ctx_0", "ctx_1", "ctx_2")
HIGH = lax.Precision.HIGHEST
MIX = 0.25
STEP = 0.1
EPS = 1e-06


def in_one_piece(arrays, axis, dim, along):
    widths = [math.prod(a.shape[along:]) for a in arrays]
    both = jnp.concatenate(
        [a.reshape(*a.shape[:along], w) for a, w in zip(arrays, widths)], axis=along
    )
    whole = lax.all_gather(both, axis, axis=dim, tiled=True)
    blocks = jnp.split(whole, [sum(widths[:k]) for k in range(1, len(widths))], axis=along)
    return tuple(
        (b.reshape(*whole.shape[:along], *a.shape[along:]) for a, b in zip(arrays, blocks))
    )


def nothing_yet(x, identity):
    return jax.tree.map(
        lambda part, zero: jnp.zeros_like(part) + jnp.asarray(zero, part.dtype), x, identity
    )


def prefix_by_axis(x, axes, combine, identity, reverse):
    before = start = nothing_yet(x, identity)
    running = x
    for axis in reversed(axes):
        size, mine = (lax.axis_size(axis), lax.axis_index(axis))
        pieces = jax.tree.map(lambda part: lax.all_gather(part, axis), running)
        inside, running = (start, start)
        for k in reversed(range(size)) if reverse else range(size):
            passed = k > mine if reverse else k < mine
            running = combine(running, jax.tree.map(lambda part: part[k], pieces))
            inside = jax.tree.map(lambda new, old: jnp.where(passed, new, old), running, inside)
        before = combine(inside, before)
    return before


def in_order(blocks, dim):
    shape = list(blocks.shape[1:])
    shape[dim] *= blocks.shape[0]
    return jnp.moveaxis(blocks, 0, dim).reshape(shape)


def gather_together(arrays, axis, dims):
    ravelled = jnp.concatenate([a.reshape(-1) for a in arrays])
    lines, at, gathered = (lax.all_gather(ravelled, axis), 0, [])
    for a, dim in zip(arrays, dims):
        blocks = lines[:, at : at + a.size].reshape(-1, *a.shape)
        gathered.append(in_order(blocks, dim))
        at += a.size
    return tuple(gathered)


def summed_rows(x, axes, dim):
    for axis in axes:
        x = lax.psum_scatter(x, axis, scatter_dimension=dim, tiled=True)
    return x


def span_pass(dt_bias, rate, state, blocks):
    xc, bc, cc, zc = blocks
    dt = jax.nn.softplus(zc + dt_bias)
    logs = -rate * dt
    cums = jnp.cumsum(logs, axis=0)
    length = xc.shape[0]
    rows = lax.broadcasted_iota(jnp.int32, (length, length), 0)
    cols = lax.broadcasted_iota(jnp.int32, (length, length), 1)
    causal = rows >= cols
    scores = jnp.einsum("ign,jgn->gij", cc, bc, precision=HIGH)
    order = jnp.transpose(cums, (1, 2, 0))
    diff = order[:, :, :, None] - order[:, :, None, :]
    decays = jnp.where(causal, jnp.exp(jnp.where(causal, diff, 0.0)), 0.0)
    weights = decays * scores[:, None] * jnp.transpose(dt, (1, 2, 0))[:, :, None, :]
    intra = jnp.einsum("ghij,jghp->ighp", weights, xc, precision=HIGH)
    inter = jnp.exp(cums)[..., None] * jnp.einsum("ign,ghpn->ighp", cc, state, precision=HIGH)
    last = cums[-1]
    tail = jnp.exp(last[None] - cums) * dt
    fresh = jnp.einsum("jghp,jgh,jgn->ghpn", xc, tail, bc, precision=HIGH)
    new_state = jnp.exp(last)[..., None, None] * state + fresh
    return (new_state, intra + inter)


def run_spans(x, b, c, z, dt_bias, rate):
    tokens, groups, heads, width = x.shape
    count = tokens // SPAN
    state0 = jnp.zeros((groups, heads, width, b.shape[-1]), jnp.float32)
    blocks = (
        x.reshape(count, SPAN, groups, heads, width),
        b.reshape(count, SPAN, groups, b.shape[-1]),
        c.reshape(count, SPAN, groups, c.shape[-1]),
        z.reshape(count, SPAN, groups, heads),
    )
    final, ys = lax.scan(partial(span_pass, dt_bias, rate), state0, blocks)
    return (ys.reshape(tokens, groups, heads, width), final)


def link(earlier, later):
    return (earlier[0] * later[0], later[0][..., None, None] * earlier[1] + later[1])


def contract_last(left, right):
    return lax.dot_general(
        left, right, (((1,), (1,)), ((), ())), preferred_element_type=jnp.float32
    )


def rwalk(weight, grad, fisher, importance):
    fisher_new = MIX * grad * grad + (1.0 - MIX) * fisher
    delta = -STEP * grad
    importance_new = importance + -grad * delta / (0.5 * fisher_new * delta * delta + EPS)
    weight_new = weight.astype(jnp.float32) + delta
    return (weight_new, fisher_new, importance_new)


def local(features, inner, w_bc, w_dt, dt_bias, decay_rate, skip, cotangent, fisher, importance):
    tokens = features.shape[0]
    groups = w_bc.shape[2] // N
    per_group = HEADS // G
    whole = lax.all_gather(features, "tp", axis=1, tiled=True)
    rows_bc, rows_dt = in_one_piece((w_bc, w_dt), CTX, 0, 1)
    depth = rows_bc.shape[0]
    wide = rows_bc.reshape(depth, 2 * groups * N)
    block_bc, block_dt = (
        lax.all_to_all(wide, "tp", split_axis=0, concat_axis=1, tiled=True),
        lax.all_to_all(rows_dt, "tp", split_axis=0, concat_axis=1, tiled=True),
    )
    proj = jnp.dot(whole, wide, preferred_element_type=jnp.float32)
    proj = lax.optimization_barrier(proj.astype(jnp.bfloat16)).astype(jnp.float32)
    bmat = proj[:, : groups * N].reshape(tokens, groups, N)
    cmat = proj[:, groups * N :].reshape(tokens, groups, N)
    zdt = jnp.dot(whole, rows_dt, preferred_element_type=jnp.float32).reshape(
        tokens, groups, per_group
    )
    bias = dt_bias.reshape(groups, per_group)
    rate = decay_rate.reshape(groups, per_group)
    gain = skip.reshape(groups, per_group)
    xval = inner.astype(jnp.float32).reshape(tokens, groups, per_group, P_SIZE)

    def zero_start(xv, bv, cv, zv):
        core, final = run_spans(xv, bv, cv, zv, bias, rate)
        return (core + gain[..., None] * xv, final)

    def enter(cv, zv, incoming):
        logs = -rate * jax.nn.softplus(zv + bias)
        cums = jnp.cumsum(logs, axis=0)
        added = jnp.exp(cums)[..., None] * jnp.einsum(
            "ign,ghpn->ighp", cv, incoming, precision=HIGH
        )
        return (added, jnp.exp(cums[-1])[..., None, None] * incoming)

    (base, local_state), back_zero = jax.vjp(zero_start, xval, bmat, cmat, zdt)
    decay = jnp.exp(jnp.sum(-rate * jax.nn.softplus(zdt + bias), axis=0))
    identity = (jnp.ones_like(decay), jnp.zeros_like(local_state))
    carried = prefix_by_axis((decay, local_state), CTX, link, identity, False)[1]
    (added, passed), back_enter = jax.vjp(enter, cmat, zdt, carried)
    outputs = (base + added).reshape(tokens, -1).astype(jnp.bfloat16)
    upstream = cotangent.astype(jnp.float32).reshape(xval.shape)
    dc_enter, dz_enter, state_local = back_enter((upstream, jnp.zeros_like(passed)))
    later = prefix_by_axis((decay, state_local), CTX, link, identity, True)[1]
    dz_pass = back_enter((jnp.zeros_like(upstream), later))[1]
    dx, dbm, dc_zero, dz_zero = back_zero((upstream, later))
    dcm = dc_zero + dc_enter
    dz = dz_zero + dz_enter + dz_pass
    grad_inner = dx.reshape(tokens, -1).astype(jnp.bfloat16)
    dproj = jnp.concatenate(
        [dbm.reshape(tokens, groups * N), dcm.reshape(tokens, groups * N)], axis=1
    ).astype(jnp.bfloat16)
    dz_half = dz.reshape(tokens, -1).astype(jnp.bfloat16)
    every_bc, every_dt = gather_together((dproj, dz_half), "tp", (1, 1))
    grad_features = (contract_last(every_bc, block_bc) + contract_last(every_dt, block_dt)).astype(
        jnp.bfloat16
    )
    product = lax.dot_general(
        whole, dproj, (((0,), (0,)), ((), ())), preferred_element_type=jnp.float32
    )
    summed = summed_rows(product, CTX, 0)
    grad = summed.reshape(w_bc.shape) / (tokens * lax.axis_size(CTX))
    weight_new, fisher_new, importance_new = rwalk(w_bc, grad, fisher, importance)
    return (outputs, grad_inner, grad_features, weight_new, fisher_new, importance_new)


def solution(mesh):
    split = Mesh(mesh.devices.reshape(4, 4, 2, mesh.shape["tp"]), ("ctx_0", "ctx_1", "ctx_2", "tp"))
    placed = (
        P(CTX, "tp"),
        P(CTX, "tp"),
        P(CTX, None, "tp"),
        P(CTX, "tp"),
        P("tp"),
        P("tp"),
        P("tp"),
        P(CTX, "tp"),
        P(CTX, None, "tp"),
        P(CTX, None, "tp"),
    )
    return jax.shard_map(
        local,
        mesh=split,
        in_specs=placed,
        out_specs=(
            P(CTX, "tp"),
            P(CTX, "tp"),
            P(CTX, "tp"),
            P(CTX, None, "tp"),
            P(CTX, None, "tp"),
            P(CTX, None, "tp"),
        ),
        check_vma=False,
    )
```

profile of v0, /device:TPU:1, one launch (start us, length us, event | category | flops | bytes accessed | tf_op | source)
XLA Modules:
  0.0 664.1 jit_solution(10560624996359038437)
XLA Ops:
  9.0 1.4 pad_maximum_fusion
  12.3 54.7 %all-gather.17.cloned.1.call-done = bf16[256,8192]{1,0:T(8,128)(2,1)} async-done(((bf16[256,1024]{1,0:T(8,128)(2,1)}), bf16[256,8192]{1,0:T(8,128)(2,1)}) %all-gather.17.cloned.1.call-update) | async-done | bytes 4194320 | tf_op jit(solution)/shard_map/all_gather | solution.py:135
  67.0 143.1 %all-gather.15.cloned.1.call-done = bf16[8192,272]{0,1:T(8,128)(2,1)} async-done(((bf16[256,272]{0,1:T(8,128)(2,1)}), bf16[8192,272]{0,1:T(8,128)(2,1)}) %all-gather.15.cloned.1.call-update) | async-done | bytes 4456464 | tf_op jit(solution)/shard_map/all_gather | solution.py:26
  210.2 3.5 fusion.246
  215.0 4.8 fusion.54
  220.0 1.4 convolution_add_fusion.1
  221.9 1.4 convolution_add_fusion
  226.1 3.8 all-reduce.3
  230.0 6.0 all-reduce.4
  236.6 29.4 %all-gather.27.cloned.1.call-done = f32[32,64,128]{2,1,0:T(8,128)} async-done(((f32[16,64,128]{2,1,0:T(8,128)}), f32[32,64,128]{2,1,0:T(8,128)}) %all-gather.27.cloned.1.call-update) | async-done | bytes 1048592 | tf_op jit(solution)/shard_map/all_gather | solution.py:44
  266.0 2.1 bitcast_add_fusion.30
  268.2 26.9 %all-gather.29.cloned.1.call-done = f32[32,64,128]{2,1,0:T(8,128)} async-done(((f32[16,64,128]{2,1,0:T(8,128)}), f32[32,64,128]{2,1,0:T(8,128)}) %all-gather.29.cloned.1.call-update) | async-done | bytes 1048592 | tf_op jit(solution)/shard_map/all_gather | solution.py:44
  295.1 2.1 bitcast_add_fusion.28
  297.9 33.2 %all-gather.19.cloned.1.call-done = f32[4,1,16,64,128]{4,3,2,1,0:T(8,128)} async-done(((f32[1,1,16,64,128]{4,3,2,1,0:T(8,128)}), f32[4,1,16,64,128]{4,3,2,1,0:T(8,128)}) %all-gather.19.cloned.1.call-update) | async-done | bytes 2097168 | tf_op jit(solution)/shard_map/all_gather | solution.py:44
  331.1 35.6 %all-gather.23.cloned.1.call-done = f32[4,1,16,64,128]{4,3,2,1,0:T(8,128)} async-done(((f32[1,1,16,64,128]{4,3,2,1,0:T(8,128)}), f32[4,1,16,64,128]{4,3,2,1,0:T(8,128)}) %all-gather.23.cloned.1.call-update) | async-done | bytes 2097168 | tf_op jit(solution)/shard_map/all_gather | solution.py:44
  366.8 3.6 multiply_add_fusion
  371.2 2.0 copy.179
  373.3 2.1 copy.192
  378.9 7.6 %all_gather.69 = f32[4,1,16]{2,1,0:T(1,128)S(1)} all-gather(f32[1,1,16]{2,1,0:T(1,128)S(1)} %get-tuple-element.452), channel_id=1, replica_groups=mesh['ctx_0'=4,'ctx_1'=4,'ctx_2'=2,'tp'=8] {'ctx_0'}, dimensions={0}, use_global_device_ids=true | all-gather | bytes 320 | tf_op jit(solution)/shard_map/all_gather | solution.py:44
  386.5 6.5 all_gather.64
  393.0 1.4 convolution_bitcast_fusion.7
  397.8 6.1 all-gather.21.cloned.1.call-done
  403.9 3.0 add_add_fusion
  407.7 1.8 convolution_bitcast_fusion.6
  409.5 30.2 %all-gather.25.cloned.1.call-done = f32[4,1,16,64,128]{4,3,2,1,0:T(8,128)} async-done(((f32[1,1,16,64,128]{4,3,2,1,0:T(8,128)}), f32[4,1,16,64,128]{4,3,2,1,0:T(8,128)}) %all-gather.25.cloned.1.call-update) | async-done | bytes 2097168 | tf_op jit(solution)/shard_map/all_gather | solution.py:44
  439.7 5.4 multiply_reduce_fusion.2
  445.0 1.5 copy.228
  446.5 2.4 fusion.245
  450.0 5.2 fusion.10
  456.0 4.1 fusion.57
  460.1 4.6 convolution_bitcast_fusion
  466.3 7.8 %all-to-all-start.1 = ((bf16[8,1024,16]{1,2,0:T(8,128)(2,1)}), bf16[8,1024,16]{1,2,0:T(8,128)(2,1)S(1)}, u32[]{:S(2)}, u32[]{:S(2)}) async-start(bf16[8,1024,16]{1,2,0:T(8,128)(2,1)} %bitcast.591), calls=%async_computation.1 | async-start | bytes 524288 | tf_op jit(solution)/shard_map/all_to_all | solution.py:141
  474.2 4.6 split.9
  478.7 6.4 copy.208
  485.9 7.3 %all-to-all-start = ((bf16[8,1024,256]{2,1,0:T(8,128)(2,1)}), bf16[8,1024,256]{2,1,0:T(8,128)(2,1)}, u32[]{:S(2)}, u32[]{:S(2)}) async-start(bf16[8,1024,256]{2,1,0:T(8,128)(2,1)} %bitcast.574), calls=%async_computation | async-start | bytes 8388608 | tf_op jit(solution)/shard_map/all_to_all | solution.py:140
  493.2 54.8 %reduce-scatter.4.cloned.1.call-done = f32[2048,256]{0,1:T(8,128)} async-done(((f32[8192,256]{0,1:T(8,128)}), f32[2048,256]{0,1:T(8,128)}) %reduce-scatter.4.cloned.1.call-update) | async-done | bytes 2097168 | tf_op jit(solution)/shard_map/reduce_scatter | solution.py:72
  548.3 1.6 convolution_bitcast_fusion.2
  550.0 2.2 multiply_reduce_fusion.5
  552.2 1.5 copy.197
  553.7 1.5 copy.202
  555.1 1.5 copy.205
  556.6 1.5 copy.198
  558.1 1.5 copy.199
  559.5 1.5 copy.195
  562.9 4.9 multiply_reduce_fusion.8
  569.2 1.6 copy.200
  570.7 3.8 reduce-window.54
  574.5 1.6 copy.203
  576.1 3.8 reduce-window.56
  579.8 1.5 copy.204
  581.3 1.4 slice_reduce_fusion.1
  583.9 1.5 copy.201
  588.0 1.6 copy.206
  589.6 3.8 reduce-window.58
  593.3 1.5 copy.207
  594.8 1.4 slice_reduce_fusion
  599.5 2.0 fusion.206
  602.4 1.6 pad_maximum_fusion.1
  605.2 5.9 fusion.50
  611.2 4.3 fusion.32
  617.8 17.2 %all-gather.31.cloned.1.call-done = bf16[557056]{0:T(1024)(128)(2,1)} async-done(((bf16[69632]{0:T(1024)(128)(2,1)}), bf16[557056]{0:T(1024)(128)(2,1)}) %all-gather.31.cloned.1.call-update) | async-done | bytes 1114128 | tf_op jit(solution)/shard_map/all_gather | solution.py:62
  635.0 1.7 reshape.2054
  638.7 4.6 fusion.47
  643.3 11.1 %reduce-scatter.8.cloned.1.call-done = f32[256,256]{0,1:T(8,128)} async-done(((f32[512,256]{0,1:T(8,128)}), f32[256,256]{0,1:T(8,128)}) %reduce-scatter.8.cloned.1.call-update) | async-done | bytes 262160 | tf_op jit(solution)/shard_map/reduce_scatter | solution.py:72
  (236 shorter events, 40.7 us)
Async XLA Ops:
  7.2 59.9 %all-gather.17.cloned.1.call-start = ((), (), s32[]{:S(2)}) async-start(), calls=%async_computation.6 | async-start | bytes 4718592 | tf_op jit(solution)/shard_map/all_gather | solution.py:135
  7.9 202.3 %all-gather.15.cloned.1.call-start = ((), (), s32[]{:S(2)}) async-start(), calls=%async_computation.5 | async-start | bytes 4595712 | tf_op jit(solution)/shard_map/all_gather | solution.py:26
  10.4 255.6 %all-gather.27.cloned.1.call-start = ((), (), s32[]{:S(2)}) async-start(), calls=%async_computation.14 | async-start | bytes 1572864 | tf_op jit(solution)/shard_map/all_gather | solution.py:44
  11.1 202.6 %copy-start.65 = (f32[16]{0:T(128)}, f32[16]{0:T(128)S(1)}, u32[]{:S(2)}) copy-start(f32[16]{0:T(128)S(1)} %neg.70) | copy-start | bytes 196
  12.3 207.7 %copy-start.5 = (f32[256,1024]{0,1:T(8,128)}, f32[256,1024]{0,1:T(8,128)S(1)}, u32[]{:S(2)}) copy-start(f32[256,1024]{0,1:T(8,128)S(1)} %copy.184) | copy-start | bytes 3145732
  213.7 6.1 copy-start.15
  214.6 231.9 %copy-start.11 = (f32[16,1,2,128]{0,3,2,1:T(8,128)}, f32[16,1,2,128]{0,3,2,1:T(8,128)S(1)}, u32[]{:S(2)}) copy-start(f32[16,1,2,128]{0,3,2,1:T(8,128)S(1)} %copy.180) | copy-start | bytes 49156
  214.7 7.0 %copy-start.19 = (f32[16,1,256]{0,2,1:T(8,128)}, f32[16,1,256]{0,2,1:T(8,128)S(1)}, u32[]{:S(2)}) copy-start(f32[16,1,256]{0,2,1:T(8,128)S(1)} %bitcast_add_fusion.43) | copy-start | bytes 49156
  215.0 6.5 copy-start.2
  219.8 235.7 %copy-start.13 = (bf16[256,256]{0,1:T(8,128)(2,1)}, bf16[256,256]{0,1:T(8,128)(2,1)S(1)}, u32[]{:S(2)}) copy-start(bf16[256,256]{0,1:T(8,128)(2,1)S(1)} %fusion.54) | copy-start | bytes 393220
  220.0 48.2 %copy-start.42 = (f32[256,16]{0,1:T(8,128)}, f32[256,16]{0,1:T(8,128)S(1)}, u32[]{:S(2)}) copy-start(f32[256,16]{0,1:T(8,128)S(1)} %copy.185) | copy-start | bytes 49156
  221.4 73.6 %all-gather.29.cloned.1.call-start = ((), (), s32[]{:S(2)}) async-start(), calls=%async_computation.15 | async-start | bytes 1572864 | tf_op jit(solution)/shard_map/all_gather | solution.py:44
  223.4 107.7 %all-gather.19.cloned.1.call-start = ((), (), s32[]{:S(2)}) async-start(), calls=%async_computation.7 | async-start | bytes 2621440 | tf_op jit(solution)/shard_map/all_gather | solution.py:44
  236.0 130.8 %copy-start.41 = (f32[64]{0:T(128)}, f32[64]{0:T(128)S(1)}, u32[]{:S(2)}) copy-start(f32[64]{0:T(128)S(1)} %all-reduce.4) | copy-start | bytes 772
  236.6 130.1 %copy-start.49 = (f32[16]{0:T(128)}, f32[16]{0:T(128)S(1)}, u32[]{:S(2)}) copy-start(f32[16]{0:T(128)S(1)} %get-tuple-element.454) | copy-start | bytes 196
  236.6 130.1 %copy-start.50 = (f32[16]{0:T(128)}, f32[16]{0:T(128)S(1)}, u32[]{:S(2)}) copy-start(f32[16]{0:T(128)S(1)} %get-tuple-element.456) | copy-start | bytes 196
  236.6 130.1 %copy-start.54 = (f32[16]{0:T(128)}, f32[16]{0:T(128)S(1)}, u32[]{:S(2)}) copy-start(f32[16]{0:T(128)S(1)} %get-tuple-element.455) | copy-start | bytes 196
  236.6 130.1 %copy-start.56 = (f32[16]{0:T(128)}, f32[16]{0:T(128)S(1)}, u32[]{:S(2)}) copy-start(f32[16]{0:T(128)S(1)} %get-tuple-element.457) | copy-start | bytes 196
  268.2 98.6 %all-gather.23.cloned.1.call-start = ((), (), s32[]{:S(2)}) async-start(), calls=%async_computation.9 | async-start | bytes 2621440 | tf_op jit(solution)/shard_map/all_gather | solution.py:44
  297.2 106.7 %all-gather.21.cloned.1.call-start = ((), (), s32[]{:S(2)}) async-start(), calls=%async_computation.8 | async-start | bytes 2621440 | tf_op jit(solution)/shard_map/all_gather | solution.py:44
  366.8 37.2 %copy-start.1 = (f32[4,1,16,64,128]{4,3,2,1,0:T(8,128)S(1)}, f32[4,1,16,64,128]{4,3,2,1,0:T(8,128)}, u32[]{:S(2)}) copy-start(f32[4,1,16,64,128]{4,3,2,1,0:T(8,128)} %all-gather.19.cloned.1.call-done) | copy-start | bytes 6291460
  370.4 69.3 %all-gather.25.cloned.1.call-start = ((), (), s32[]{:S(2)}) async-start(), calls=%async_computation.10 | async-start | bytes 2621440 | tf_op jit(solution)/shard_map/all_gather | solution.py:44
  371.2 176.9 %reduce-scatter.4.cloned.1.call-start = ((), (), s32[]{:S(2)}) async-start(), calls=%async_computation.11 | async-start | bytes 10485760 | tf_op jit(solution)/shard_map/reduce_scatter | solution.py:72
  449.8 5.6 copy-start.24
  449.8 5.6 copy-start.32
  449.9 5.9 copy-start.6
  449.9 5.9 copy-start.10
  449.9 5.9 copy-start.17
  449.9 5.9 copy-start.18
  449.9 5.9 copy-start.43
  449.9 5.9 copy-start.51
  449.9 5.9 copy-start.52
  449.9 5.9 copy-start.55
  449.9 5.9 copy-start.57
  450.0 5.9 copy-start.58
  450.0 5.9 copy-start.59
  450.0 5.9 copy-start.60
  450.0 5.9 copy-start.61
  450.0 5.9 copy-start.63
  450.0 5.9 copy-start.64
  456.0 8.7 %copy-start.22 = (bf16[256,128]{0,1:T(8,128)(2,1)}, bf16[256,128]{0,1:T(8,128)(2,1)S(1)}, u32[]{:S(2)}) copy-start(bf16[256,128]{0,1:T(8,128)(2,1)S(1)} %fusion.55) | copy-start | bytes 196612
  466.3 18.8 %all-to-all-start.1 = ((bf16[8,1024,16]{1,2,0:T(8,128)(2,1)}), bf16[8,1024,16]{1,2,0:T(8,128)(2,1)S(1)}, u32[]{:S(2)}, u32[]{:S(2)}) async-start(bf16[8,1024,16]{1,2,0:T(8,128)(2,1)} %bitcast.591), calls=%async_computation.1 | async-start | bytes 524288 | tf_op jit(solution)/shard_map/all_to_all | solution.py:141
  485.9 62.5 %copy-start.14 = (bf16[256,256]{0,1:T(8,128)(2,1)S(1)}, bf16[256,256]{0,1:T(8,128)(2,1)}, u32[]{:S(2)}) copy-start(bf16[256,256]{0,1:T(8,128)(2,1)} %copy-done.13) | copy-start | bytes 393220
  485.9 152.8 %all-to-all-start = ((bf16[8,1024,256]{2,1,0:T(8,128)(2,1)}), bf16[8,1024,256]{2,1,0:T(8,128)(2,1)}, u32[]{:S(2)}, u32[]{:S(2)}) async-start(bf16[8,1024,256]{2,1,0:T(8,128)(2,1)} %bitcast.574), calls=%async_computation | async-start | bytes 8388608 | tf_op jit(solution)/shard_map/all_to_all | solution.py:140
  493.2 67.8 %copy-start.23 = (bf16[256,128]{0,1:T(8,128)(2,1)S(1)}, bf16[256,128]{0,1:T(8,128)(2,1)}, u32[]{:S(2)}) copy-start(bf16[256,128]{0,1:T(8,128)(2,1)} %copy-done.22) | copy-start | bytes 196612
  493.2 67.8 %copy-start.34 = (bf16[256,128]{0,1:T(8,128)(2,1)S(1)}, bf16[256,128]{0,1:T(8,128)(2,1)}, u32[]{:S(2)}) copy-start(bf16[256,128]{0,1:T(8,128)(2,1)} %copy-done.33) | copy-start | bytes 196612
  493.2 117.9 %reduce-scatter.6.cloned.1.call-start = ((), (), s32[]{:S(2)}) async-start(), calls=%async_computation.12 | async-start | bytes 2621440 | tf_op jit(solution)/shard_map/reduce_scatter | solution.py:72
  548.1 86.9 %all-gather.31.cloned.1.call-start = ((), (), s32[]{:S(2)}) async-start(), calls=%async_computation.16 | async-start | bytes 1253376 | tf_op jit(solution)/shard_map/all_gather | solution.py:62
  562.9 36.6 %copy-start.12 = (f32[16,1,2,128]{0,3,2,1:T(8,128)S(1)}, f32[16,1,2,128]{0,3,2,1:T(8,128)}, u32[]{:S(2)}) copy-start(f32[16,1,2,128]{0,3,2,1:T(8,128)} %copy-done.11) | copy-start | bytes 49156
  562.9 36.6 %copy-start.16 = (f32[256,16]{1,0:T(8,128)S(1)}, f32[256,16]{1,0:T(8,128)}, u32[]{:S(2)}) copy-start(f32[256,16]{1,0:T(8,128)} %copy-done.15) | copy-start | bytes 49156
  567.8 37.3 %copy-start.7 = (f32[256,1024]{0,1:T(8,128)S(1)}, f32[256,1024]{0,1:T(8,128)}, u32[]{:S(2)}) copy-start(f32[256,1024]{0,1:T(8,128)} %copy-done.5) | copy-start | bytes 3145732
  567.8 37.3 %copy-start.9 = (f32[256,1,16,64]{0,3,2,1:T(8,128)S(1)}, f32[256,1,16,64]{0,3,2,1:T(8,128)}, u32[]{:S(2)}) copy-start(f32[256,1,16,64]{0,3,2,1:T(8,128)} %copy-done.8) | copy-start | bytes 3145732
  567.8 37.3 %copy-start.21 = (f32[256,1,16,64]{0,3,2,1:T(8,128)S(1)}, f32[256,1,16,64]{0,3,2,1:T(8,128)}, u32[]{:S(2)}) copy-start(f32[256,1,16,64]{0,3,2,1:T(8,128)} %get-tuple-element.467) | copy-start | bytes 3145732
  604.0 50.4 %reduce-scatter.8.cloned.1.call-start = ((), (), s32[]{:S(2)}) async-start(), calls=%async_computation.13 | async-start | bytes 786432 | tf_op jit(solution)/shard_map/reduce_scatter | solution.py:72
  605.1 6.0 copy-start.37
  605.1 6.0 copy-start.44
  605.2 6.0 copy-start.45
  605.2 6.0 copy-start.46
  605.2 6.0 copy-start.48
  611.2 5.7 copy-start.3
  615.8 21.5 %copy-start.40 = (bf16[8,1024,16]{1,2,0:T(8,128)(2,1)S(1)}, bf16[8,1024,16]{1,2,0:T(8,128)(2,1)}, u32[]{:S(2)}) copy-start(bf16[8,1024,16]{1,2,0:T(8,128)(2,1)} %copy-done.39) | copy-start | bytes 786436
  638.7 17.2 %copy-start.25 = (bf16[256,2,128]{2,1,0:T(2,128)(2,1)S(1)}, bf16[256,2,128]{2,1,0:T(2,128)(2,1)}, u32[]{:S(2)}) copy-start(bf16[256,2,128]{2,1,0:T(2,128)(2,1)} %param.12) | copy-start | bytes 393220
  638.7 17.2 %copy-start.35 = (f32[256,2,128]{2,1,0:T(2,128)S(1)}, f32[256,2,128]{2,1,0:T(2,128)}, u32[]{:S(2)}) copy-start(f32[256,2,128]{2,1,0:T(2,128)} %param.19) | copy-start | bytes 786436
  638.7 17.2 %copy-start.36 = (f32[256,2,128]{2,1,0:T(2,128)S(1)}, f32[256,2,128]{2,1,0:T(2,128)}, u32[]{:S(2)}) copy-start(f32[256,2,128]{2,1,0:T(2,128)} %param.18) | copy-start | bytes 786436
  (19 other events, 72.9 us)
Sparse Core Ops, SparseCore 0:
  9.8 57.1 all-gather.16
  69.3 140.8 all-gather.14
  221.6 44.3 all-gather.26
  268.2 26.8 all-gather.28
  297.3 33.7 all-gather.18
  333.3 33.3 all-gather.22
  370.5 33.3 all-gather.20
  406.3 33.3 all-gather.24
  464.8 83.1 reduce-scatter.3
  550.4 32.0 reduce-scatter.5
  604.1 30.7 all-gather.30
  637.3 17.0 reduce-scatter.7
where the time goes:
time: 666 us; the launch traced here: 664 us
  waiting for transfers between devices  444 us (67%)
  local copies, waits for them, and re-layouts  58.3 us (9%)
  matrix products  55 us (8%)
  other arithmetic  50.5 us (8%)
  blocking collectives  23.8 us (4%)
  between operations  16.6 us (2%)
  starting transfers between devices  16.1 us (2%)
    all_gather x6, waiting for transfers between devices, prefix_by_axis(): pieces = jax.tree.map(lambda part: lax.all_gather(part, axis), running)  161 us
    all_gather x1, waiting for transfers between devices, in_one_piece(): whole = lax.all_gather(both, axis, axis=dim, tiled=True)  143 us
    reduce_scatter x3, waiting for transfers between devices, summed_rows(): x = lax.psum_scatter(x, axis, scatter_dimension=dim, tiled=True)  65.9 us
    all_gather x1, waiting for transfers between devices, local(): whole = lax.all_gather(features, 'tp', axis=1, tiled=True)  54.7 us
    another operation x23, local copies, waits for them, and re-layouts  17.6 us
    all_gather x1, waiting for transfers between devices, gather_together(): lines, at, gathered = (lax.all_gather(ravelled, axis), 0, [])  17.2 us
    another operation x9, other arithmetic  15.8 us
    dot_general x3, matrix products, span_pass(): intra = jnp.einsum('ghij,jghp->ighp', weights, xc, precision=HIGH)  15.4 us
  transfers between devices with their start and end apart: 14, of which 11 were waited for; matrix products, arithmetic and copies ran while one was open for 18% of the time, Pallas kernels for 0%

commit v1 on v0

--- a/solution.py
+++ b/solution.py
@@ -132,7 +132,10 @@
     tokens = features.shape[0]
     groups = w_bc.shape[2] // N
     per_group = HEADS // G
-    whole = lax.all_gather(features, "tp", axis=1, tiled=True)
+    devices = lax.axis_size("tp")
+    parts = jnp.stack([features for _ in range(devices)])
+    parts = lax.all_to_all(parts, "tp", split_axis=0, concat_axis=0)
+    whole = jnp.concatenate(parts, axis=1)
     rows_bc, rows_dt = in_one_piece((w_bc, w_dt), CTX, 0, 1)
     depth = rows_bc.shape[0]
     wide = rows_bc.reshape(depth, 2 * groups * N)

time: 666 us -> 682 us (1.024)
  starting transfers between devices: 16.1 us -> 26.1 us
    all_to_all x0 -> x1, waiting for transfers between devices: none -> 132 us  [local(): parts = lax.all_to_all(parts, 'tp', split_axis=0, concat_axis=0)]
    all_gather x1, waiting for transfers between devices: 143 us -> 73.6 us  [in_one_piece(): whole = lax.all_gather(both, axis, axis=dim, tiled=True)]
    all_gather x1 -> x0, waiting for transfers between devices: 54.7 us -> none  [local(): whole = lax.all_gather(features, 'tp', axis=1, tiled=True)]
    all_to_all x0 -> x1, starting transfers between devices: none -> 10.1 us  [local(): parts = lax.all_to_all(parts, 'tp', split_axis=0, concat_axis=0)]
    another operation x23 -> x24, local copies, waits for them, and re-layouts: 17.6 us -> 19.8 us
  transfers between devices with their start and end apart: 14 -> 14, of which waited for: 11 -> 11; matrix products, arithmetic and copies ran while one was open for 18% -> 17% of each run, Pallas kernels for 0% -> 0%
where the time goes in v1:
time: 682 us; the launch traced here: 679 us
  waiting for transfers between devices  445 us (65%)
  local copies, waits for them, and re-layouts  61 us (9%)
  matrix products  56.9 us (8%)
  other arithmetic  49.8 us (7%)
  starting transfers between devices  26.1 us (4%)
  blocking collectives  24.2 us (4%)
  between operations  16.3 us (2%)
    all_gather x6, waiting for transfers between devices, prefix_by_axis(): pieces = jax.tree.map(lambda part: lax.all_gather(part, axis), running)  155 us
    all_to_all x1, waiting for transfers between devices, local(): parts = lax.all_to_all(parts, 'tp', split_axis=0, concat_axis=0)  132 us
    all_gather x1, waiting for transfers between devices, in_one_piece(): whole = lax.all_gather(both, axis, axis=dim, tiled=True)  73.6 us
    reduce_scatter x3, waiting for transfers between devices, summed_rows(): x = lax.psum_scatter(x, axis, scatter_dimension=dim, tiled=True)  66.1 us
    another operation x23, local copies, waits for them, and re-layouts  17.6 us
    all_gather x1, waiting for transfers between devices, gather_together(): lines, at, gathered = (lax.all_gather(ravelled, axis), 0, [])  17.2 us
    another operation x9, other arithmetic  15.8 us
    dot_general x3, matrix products, span_pass(): intra = jnp.einsum('ghij,jghp->ighp', weights, xc, precision=HIGH)  15.4 us
  transfers between devices with their start and end apart: 14, of which 11 were waited for; matrix products, arithmetic and copies ran while one was open for 17% of the time, Pallas kernels for 0%

profile of v1, /device:TPU:1, one launch (start us, length us, event | category | flops | bytes accessed | tf_op | source)
XLA Modules:
  0.0 679.2 jit_solution(15186149813566624386)
XLA Ops:
  10.9 2.2 stack.2
  13.1 10.1 %all-to-all-start = ((bf16[8,256,1024]{1,2,0:T(8,128)(2,1)}), bf16[8,256,1024]{1,2,0:T(8,128)(2,1)}, u32[]{:S(2)}, u32[]{:S(2)}) async-start(bf16[8,256,1024]{1,2,0:T(8,128)(2,1)} %stack.2), calls=%async_computation | async-start | bytes 8388608 | tf_op jit(solution)/shard_map/all_to_all | solution.py:137
  23.5 132.4 %all-to-all-done = bf16[8,256,1024]{1,2,0:T(8,128)(2,1)} async-done(((bf16[8,256,1024]{1,2,0:T(8,128)(2,1)}), bf16[8,256,1024]{1,2,0:T(8,128)(2,1)}, u32[]{:S(2)}, u32[]{:S(2)}) %all-to-all-start) | async-done | bytes 4194336 | tf_op jit(solution)/shard_map/all_to_all | solution.py:137
  155.9 73.6 %all-gather.14.cloned.1.call-done = bf16[8192,272]{0,1:T(8,128)(2,1)} async-done(((bf16[256,272]{0,1:T(8,128)(2,1)}), bf16[8192,272]{0,1:T(8,128)(2,1)}) %all-gather.14.cloned.1.call-update) | async-done | bytes 4456464 | tf_op jit(solution)/shard_map/all_gather | solution.py:26
  229.5 3.6 fusion.246
  234.1 4.8 fusion.54
  239.2 1.4 convolution_add_fusion
  241.7 1.4 convolution_add_fusion.1
  245.8 3.8 all-reduce.3
  249.7 6.3 all-reduce.4
  256.8 22.5 %all-gather.26.cloned.1.call-done = f32[32,64,128]{2,1,0:T(8,128)} async-done(((f32[16,64,128]{2,1,0:T(8,128)}), f32[32,64,128]{2,1,0:T(8,128)}) %all-gather.26.cloned.1.call-update) | async-done | bytes 1048592 | tf_op jit(solution)/shard_map/all_gather | solution.py:44
  279.3 2.1 bitcast_add_fusion.28
  281.5 27.0 %all-gather.24.cloned.1.call-done = f32[32,64,128]{2,1,0:T(8,128)} async-done(((f32[16,64,128]{2,1,0:T(8,128)}), f32[32,64,128]{2,1,0:T(8,128)}) %all-gather.24.cloned.1.call-update) | async-done | bytes 1048592 | tf_op jit(solution)/shard_map/all_gather | solution.py:44
  308.5 2.1 bitcast_add_fusion.30
  311.4 33.1 %all-gather.20.cloned.1.call-done = f32[4,1,16,64,128]{4,3,2,1,0:T(8,128)} async-done(((f32[1,1,16,64,128]{4,3,2,1,0:T(8,128)}), f32[4,1,16,64,128]{4,3,2,1,0:T(8,128)}) %all-gather.20.cloned.1.call-update) | async-done | bytes 2097168 | tf_op jit(solution)/shard_map/all_gather | solution.py:44
  344.5 35.6 %all-gather.16.cloned.1.call-done = f32[4,1,16,64,128]{4,3,2,1,0:T(8,128)} async-done(((f32[1,1,16,64,128]{4,3,2,1,0:T(8,128)}), f32[4,1,16,64,128]{4,3,2,1,0:T(8,128)}) %all-gather.16.cloned.1.call-update) | async-done | bytes 2097168 | tf_op jit(solution)/shard_map/all_gather | solution.py:44
  380.2 3.6 multiply_add_fusion
  384.7 2.0 copy.183
  386.7 2.0 copy.196
  392.3 7.6 %all_gather.65 = f32[4,1,16]{2,1,0:T(1,128)S(1)} all-gather(f32[1,1,16]{2,1,0:T(1,128)S(1)} %get-tuple-element.452), channel_id=1, replica_groups=mesh['ctx_0'=4,'ctx_1'=4,'ctx_2'=2,'tp'=8] {'ctx_0'}, dimensions={0}, use_global_device_ids=true | all-gather | bytes 320 | tf_op jit(solution)/shard_map/all_gather | solution.py:44
  400.0 6.5 all_gather.60
  406.4 1.4 convolution_bitcast_fusion.7
  411.3 6.1 all-gather.18.cloned.1.call-done
  417.4 3.0 add_add_fusion
  421.2 1.8 convolution_bitcast_fusion.6
  423.0 30.2 %all-gather.22.cloned.1.call-done = f32[4,1,16,64,128]{4,3,2,1,0:T(8,128)} async-done(((f32[1,1,16,64,128]{4,3,2,1,0:T(8,128)}), f32[4,1,16,64,128]{4,3,2,1,0:T(8,128)}) %all-gather.22.cloned.1.call-update) | async-done | bytes 2097168 | tf_op jit(solution)/shard_map/all_gather | solution.py:44
  453.2 5.4 multiply_reduce_fusion.2
  458.5 1.5 copy.232
  460.0 2.3 fusion.245
  463.5 5.2 fusion.10
  469.4 3.7 fusion.57
  473.1 6.8 convolution_bitcast_fusion
  481.6 7.8 %all-to-all-start.2 = ((bf16[8,1024,16]{1,2,0:T(8,128)(2,1)}), bf16[8,1024,16]{1,2,0:T(8,128)(2,1)S(1)}, u32[]{:S(2)}, u32[]{:S(2)}) async-start(bf16[8,1024,16]{1,2,0:T(8,128)(2,1)} %bitcast.594), calls=%async_computation.2 | async-start | bytes 524288 | tf_op jit(solution)/shard_map/all_to_all | solution.py:144
  489.4 4.6 split.9
  494.0 6.4 copy.212
  501.1 7.3 %all-to-all-start.1 = ((bf16[8,1024,256]{2,1,0:T(8,128)(2,1)}), bf16[8,1024,256]{2,1,0:T(8,128)(2,1)}, u32[]{:S(2)}, u32[]{:S(2)}) async-start(bf16[8,1024,256]{2,1,0:T(8,128)(2,1)} %bitcast.577), calls=%async_computation.1 | async-start | bytes 8388608 | tf_op jit(solution)/shard_map/all_to_all | solution.py:143
  508.5 54.8 %reduce-scatter.4.cloned.1.call-done = f32[2048,256]{0,1:T(8,128)} async-done(((f32[8192,256]{0,1:T(8,128)}), f32[2048,256]{0,1:T(8,128)}) %reduce-scatter.4.cloned.1.call-update) | async-done | bytes 2097168 | tf_op jit(solution)/shard_map/reduce_scatter | solution.py:72
  563.6 1.6 convolution_bitcast_fusion.2
  565.2 2.2 multiply_reduce_fusion.5
  567.5 1.5 copy.201
  568.9 1.5 copy.206
  570.4 1.5 copy.209
  571.9 1.5 copy.202
  573.3 1.5 copy.203
  574.8 1.5 copy.199
  578.2 4.9 multiply_reduce_fusion.8
  584.4 1.6 copy.204
  586.0 3.8 reduce-window.54
  589.7 1.6 copy.207
  591.3 3.8 reduce-window.56
  595.1 1.5 copy.208
  599.1 1.5 copy.205
  603.3 1.6 copy.210
  604.8 3.8 reduce-window.58
  608.6 1.5 copy.211
  610.1 1.4 slice_reduce_fusion
  614.7 2.0 fusion.206
  617.6 1.6 pad_maximum_fusion.1
  620.4 5.9 fusion.50
  626.4 4.3 fusion.32
  633.0 17.2 %all-gather.28.cloned.1.call-done = bf16[557056]{0:T(1024)(128)(2,1)} async-done(((bf16[69632]{0:T(1024)(128)(2,1)}), bf16[557056]{0:T(1024)(128)(2,1)}) %all-gather.28.cloned.1.call-update) | async-done | bytes 1114128 | tf_op jit(solution)/shard_map/all_gather | solution.py:62
  650.3 1.7 reshape.2064
  654.0 4.6 fusion.47
  658.6 11.2 %reduce-scatter.8.cloned.1.call-done = f32[256,256]{0,1:T(8,128)} async-done(((f32[512,256]{0,1:T(8,128)}), f32[256,256]{0,1:T(8,128)}) %reduce-scatter.8.cloned.1.call-update) | async-done | bytes 262160 | tf_op jit(solution)/shard_map/reduce_scatter | solution.py:72
  (241 shorter events, 42.5 us)
Async XLA Ops:
  7.2 222.3 %all-gather.14.cloned.1.call-start = ((), (), s32[]{:S(2)}) async-start(), calls=%async_computation.6 | async-start | bytes 4595712 | tf_op jit(solution)/shard_map/all_gather | solution.py:26
  13.1 10.1 %copy-start.67 = (f32[16]{0:T(128)S(1)}, f32[16]{0:T(128)}, u32[]{:S(2)}) copy-start(f32[16]{0:T(128)} %param.15) | copy-start | bytes 196
  13.1 10.1 %copy-start.1 = (bf16[256,1024]{1,0:T(8,128)(2,1)S(1)}, bf16[256,1024]{1,0:T(8,128)(2,1)}, u32[]{:S(2)}) copy-start(bf16[256,1024]{1,0:T(8,128)(2,1)} %param.17) | copy-start | bytes 1572868
  13.1 216.4 %copy-start.66 = (f32[16]{0:T(128)S(1)}, f32[16]{0:T(128)}, u32[]{:S(2)}) copy-start(f32[16]{0:T(128)} %param.14) | copy-start | bytes 196
  13.1 142.7 %all-to-all-start = ((bf16[8,256,1024]{1,2,0:T(8,128)(2,1)}), bf16[8,256,1024]{1,2,0:T(8,128)(2,1)}, u32[]{:S(2)}, u32[]{:S(2)}) async-start(bf16[8,256,1024]{1,2,0:T(8,128)(2,1)} %stack.2), calls=%async_computation | async-start | bytes 8388608 | tf_op jit(solution)/shard_map/all_to_all | solution.py:137
  23.2 256.1 %all-gather.26.cloned.1.call-start = ((), (), s32[]{:S(2)}) async-start(), calls=%async_computation.15 | async-start | bytes 1572864 | tf_op jit(solution)/shard_map/all_gather | solution.py:44
  23.2 215.6 %copy-start.65 = (f32[16]{0:T(128)}, f32[16]{0:T(128)S(1)}, u32[]{:S(2)}) copy-start(f32[16]{0:T(128)S(1)} %neg.70) | copy-start | bytes 196
  233.1 7.8 %copy-start.15 = (f32[256,16]{1,0:T(8,128)}, f32[256,16]{1,0:T(8,128)S(1)}, u32[]{:S(2)}) copy-start(f32[256,16]{1,0:T(8,128)S(1)} %get-tuple-element.464) | copy-start | bytes 49156
  234.0 225.9 %copy-start.10 = (f32[16,1,2,128]{0,3,2,1:T(8,128)}, f32[16,1,2,128]{0,3,2,1:T(8,128)S(1)}, u32[]{:S(2)}) copy-start(f32[16,1,2,128]{0,3,2,1:T(8,128)S(1)} %copy.184) | copy-start | bytes 49156
  234.1 6.7 copy-start.14
  238.9 230.1 %copy-start.12 = (bf16[256,256]{0,1:T(8,128)(2,1)}, bf16[256,256]{0,1:T(8,128)(2,1)S(1)}, u32[]{:S(2)}) copy-start(bf16[256,256]{0,1:T(8,128)(2,1)S(1)} %fusion.54) | copy-start | bytes 393220
  239.0 42.5 %copy-start.19 = (f32[16,1,256]{0,2,1:T(8,128)}, f32[16,1,256]{0,2,1:T(8,128)S(1)}, u32[]{:S(2)}) copy-start(f32[16,1,256]{0,2,1:T(8,128)S(1)} %bitcast_add_fusion.43) | copy-start | bytes 49156
  240.7 67.9 %all-gather.24.cloned.1.call-start = ((), (), s32[]{:S(2)}) async-start(), calls=%async_computation.14 | async-start | bytes 1572864 | tf_op jit(solution)/shard_map/all_gather | solution.py:44
  240.9 139.2 %copy-start.4 = (f32[256,1024]{0,1:T(8,128)}, f32[256,1024]{0,1:T(8,128)S(1)}, u32[]{:S(2)}) copy-start(f32[256,1024]{0,1:T(8,128)S(1)} %copy.188) | copy-start | bytes 3145732
  241.7 138.5 %copy-start.42 = (f32[256,16]{0,1:T(8,128)}, f32[256,16]{0,1:T(8,128)S(1)}, u32[]{:S(2)}) copy-start(f32[256,16]{0,1:T(8,128)S(1)} %copy.189) | copy-start | bytes 49156
  243.1 101.4 %all-gather.20.cloned.1.call-start = ((), (), s32[]{:S(2)}) async-start(), calls=%async_computation.9 | async-start | bytes 2621440 | tf_op jit(solution)/shard_map/all_gather | solution.py:44
  256.1 124.1 %copy-start.41 = (f32[64]{0:T(128)}, f32[64]{0:T(128)S(1)}, u32[]{:S(2)}) copy-start(f32[64]{0:T(128)S(1)} %all-reduce.4) | copy-start | bytes 772
  256.7 123.5 %copy-start.49 = (f32[16]{0:T(128)}, f32[16]{0:T(128)S(1)}, u32[]{:S(2)}) copy-start(f32[16]{0:T(128)S(1)} %get-tuple-element.454) | copy-start | bytes 196
  256.7 123.5 %copy-start.50 = (f32[16]{0:T(128)}, f32[16]{0:T(128)S(1)}, u32[]{:S(2)}) copy-start(f32[16]{0:T(128)S(1)} %get-tuple-element.456) | copy-start | bytes 196
  256.7 123.5 %copy-start.54 = (f32[16]{0:T(128)}, f32[16]{0:T(128)S(1)}, u32[]{:S(2)}) copy-start(f32[16]{0:T(128)S(1)} %get-tuple-element.455) | copy-start | bytes 196
  256.8 123.5 %copy-start.56 = (f32[16]{0:T(128)}, f32[16]{0:T(128)S(1)}, u32[]{:S(2)}) copy-start(f32[16]{0:T(128)S(1)} %get-tuple-element.457) | copy-start | bytes 196
  281.5 98.7 %all-gather.16.cloned.1.call-start = ((), (), s32[]{:S(2)}) async-start(), calls=%async_computation.7 | async-start | bytes 2621440 | tf_op jit(solution)/shard_map/all_gather | solution.py:44
  310.7 106.7 %all-gather.18.cloned.1.call-start = ((), (), s32[]{:S(2)}) async-start(), calls=%async_computation.8 | async-start | bytes 2621440 | tf_op jit(solution)/shard_map/all_gather | solution.py:44
  380.2 37.2 %copy-start = (f32[4,1,16,64,128]{4,3,2,1,0:T(8,128)S(1)}, f32[4,1,16,64,128]{4,3,2,1,0:T(8,128)}, u32[]{:S(2)}) copy-start(f32[4,1,16,64,128]{4,3,2,1,0:T(8,128)} %all-gather.16.cloned.1.call-done) | copy-start | bytes 6291460
  383.9 69.3 %all-gather.22.cloned.1.call-start = ((), (), s32[]{:S(2)}) async-start(), calls=%async_computation.10 | async-start | bytes 2621440 | tf_op jit(solution)/shard_map/all_gather | solution.py:44
  384.6 178.7 %reduce-scatter.4.cloned.1.call-start = ((), (), s32[]{:S(2)}) async-start(), calls=%async_computation.11 | async-start | bytes 10485760 | tf_op jit(solution)/shard_map/reduce_scatter | solution.py:72
  463.3 5.9 copy-start.5
  463.3 5.9 copy-start.9
  463.3 5.9 copy-start.17
  463.3 5.9 copy-start.18
  463.4 5.9 copy-start.43
  463.4 5.9 copy-start.51
  463.4 5.9 copy-start.52
  463.4 5.9 copy-start.55
  463.4 5.9 copy-start.57
  463.4 5.9 copy-start.58
  463.4 5.9 copy-start.59
  463.4 5.9 copy-start.60
  463.4 5.9 copy-start.61
  463.4 5.9 copy-start.63
  469.4 10.5 %copy-start.22 = (bf16[256,128]{0,1:T(8,128)(2,1)}, bf16[256,128]{0,1:T(8,128)(2,1)S(1)}, u32[]{:S(2)}) copy-start(bf16[256,128]{0,1:T(8,128)(2,1)S(1)} %fusion.55) | copy-start | bytes 196612
  473.1 6.8 %copy-start.33 = (bf16[256,128]{0,1:T(8,128)(2,1)}, bf16[256,128]{0,1:T(8,128)(2,1)S(1)}, u32[]{:S(2)}) copy-start(bf16[256,128]{0,1:T(8,128)(2,1)S(1)} %fusion.57) | copy-start | bytes 196612
  481.6 18.8 %all-to-all-start.2 = ((bf16[8,1024,16]{1,2,0:T(8,128)(2,1)}), bf16[8,1024,16]{1,2,0:T(8,128)(2,1)S(1)}, u32[]{:S(2)}, u32[]{:S(2)}) async-start(bf16[8,1024,16]{1,2,0:T(8,128)(2,1)} %bitcast.594), calls=%async_computation.2 | async-start | bytes 524288 | tf_op jit(solution)/shard_map/all_to_all | solution.py:144
  501.1 62.5 %copy-start.13 = (bf16[256,256]{0,1:T(8,128)(2,1)S(1)}, bf16[256,256]{0,1:T(8,128)(2,1)}, u32[]{:S(2)}) copy-start(bf16[256,256]{0,1:T(8,128)(2,1)} %copy-done.12) | copy-start | bytes 393220
  501.1 152.8 %all-to-all-start.1 = ((bf16[8,1024,256]{2,1,0:T(8,128)(2,1)}), bf16[8,1024,256]{2,1,0:T(8,128)(2,1)}, u32[]{:S(2)}, u32[]{:S(2)}) async-start(bf16[8,1024,256]{2,1,0:T(8,128)(2,1)} %bitcast.577), calls=%async_computation.1 | async-start | bytes 8388608 | tf_op jit(solution)/shard_map/all_to_all | solution.py:143
  508.4 67.8 %copy-start.23 = (bf16[256,128]{0,1:T(8,128)(2,1)S(1)}, bf16[256,128]{0,1:T(8,128)(2,1)}, u32[]{:S(2)}) copy-start(bf16[256,128]{0,1:T(8,128)(2,1)} %copy-done.22) | copy-start | bytes 196612
  508.4 67.8 %copy-start.34 = (bf16[256,128]{0,1:T(8,128)(2,1)S(1)}, bf16[256,128]{0,1:T(8,128)(2,1)}, u32[]{:S(2)}) copy-start(bf16[256,128]{0,1:T(8,128)(2,1)} %copy-done.33) | copy-start | bytes 196612
  508.4 117.8 %reduce-scatter.6.cloned.1.call-start = ((), (), s32[]{:S(2)}) async-start(), calls=%async_computation.12 | async-start | bytes 2621440 | tf_op jit(solution)/shard_map/reduce_scatter | solution.py:72
  563.3 86.9 %all-gather.28.cloned.1.call-start = ((), (), s32[]{:S(2)}) async-start(), calls=%async_computation.16 | async-start | bytes 1253376 | tf_op jit(solution)/shard_map/all_gather | solution.py:62
  578.1 36.6 %copy-start.11 = (f32[16,1,2,128]{0,3,2,1:T(8,128)S(1)}, f32[16,1,2,128]{0,3,2,1:T(8,128)}, u32[]{:S(2)}) copy-start(f32[16,1,2,128]{0,3,2,1:T(8,128)} %copy-done.10) | copy-start | bytes 49156
  578.1 36.6 %copy-start.16 = (f32[256,16]{1,0:T(8,128)S(1)}, f32[256,16]{1,0:T(8,128)}, u32[]{:S(2)}) copy-start(f32[256,16]{1,0:T(8,128)} %copy-done.15) | copy-start | bytes 49156
  583.0 37.3 %copy-start.6 = (f32[256,1024]{0,1:T(8,128)S(1)}, f32[256,1024]{0,1:T(8,128)}, u32[]{:S(2)}) copy-start(f32[256,1024]{0,1:T(8,128)} %copy-done.4) | copy-start | bytes 3145732
  583.1 37.3 %copy-start.8 = (f32[256,1,16,64]{0,3,2,1:T(8,128)S(1)}, f32[256,1,16,64]{0,3,2,1:T(8,128)}, u32[]{:S(2)}) copy-start(f32[256,1,16,64]{0,3,2,1:T(8,128)} %copy-done.7) | copy-start | bytes 3145732
  583.1 37.3 %copy-start.21 = (f32[256,1,16,64]{0,3,2,1:T(8,128)S(1)}, f32[256,1,16,64]{0,3,2,1:T(8,128)}, u32[]{:S(2)}) copy-start(f32[256,1,16,64]{0,3,2,1:T(8,128)} %get-tuple-element.467) | copy-start | bytes 3145732
  619.2 50.6 %reduce-scatter.8.cloned.1.call-start = ((), (), s32[]{:S(2)}) async-start(), calls=%async_computation.13 | async-start | bytes 786432 | tf_op jit(solution)/shard_map/reduce_scatter | solution.py:72
  620.3 6.0 copy-start.37
  620.4 6.0 copy-start.44
  620.4 6.0 copy-start.45
  620.4 6.0 copy-start.46
  620.4 6.0 copy-start.48
  631.0 21.6 %copy-start.40 = (bf16[8,1024,16]{1,2,0:T(8,128)(2,1)S(1)}, bf16[8,1024,16]{1,2,0:T(8,128)(2,1)}, u32[]{:S(2)}) copy-start(bf16[8,1024,16]{1,2,0:T(8,128)(2,1)} %copy-done.39) | copy-start | bytes 786436
  654.0 17.4 %copy-start.25 = (bf16[256,2,128]{2,1,0:T(2,128)(2,1)S(1)}, bf16[256,2,128]{2,1,0:T(2,128)(2,1)}, u32[]{:S(2)}) copy-start(bf16[256,2,128]{2,1,0:T(2,128)(2,1)} %param.12) | copy-start | bytes 393220
  654.0 17.4 %copy-start.35 = (f32[256,2,128]{2,1,0:T(2,128)S(1)}, f32[256,2,128]{2,1,0:T(2,128)}, u32[]{:S(2)}) copy-start(f32[256,2,128]{2,1,0:T(2,128)} %param.19) | copy-start | bytes 786436
  654.0 17.4 %copy-start.36 = (f32[256,2,128]{2,1,0:T(2,128)S(1)}, f32[256,2,128]{2,1,0:T(2,128)}, u32[]{:S(2)}) copy-start(f32[256,2,128]{2,1,0:T(2,128)} %param.18) | copy-start | bytes 786436
  (21 other events, 87.8 us)
Sparse Core Ops, SparseCore 0:
  10.3 219.1 all-gather.13
  240.8 38.4 all-gather.25
  281.7 26.8 all-gather.23
  310.8 33.7 all-gather.19
  346.8 33.3 all-gather.15
  384.0 33.3 all-gather.17
  419.8 33.3 all-gather.21
  480.1 83.1 reduce-scatter.3
  565.9 32.0 reduce-scatter.5
  619.3 30.8 all-gather.27
  652.8 17.0 reduce-scatter.7
